TPU v7x, 32 devices: a whole 2x2x4 slice. The times are simulated.
32 devices in a mesh: seq: 16 (over z, y, x), wa: 2 (over core).
Axes of the slice: x: 2, y: 2, z: 4, core: 2. Of those that a mesh axis runs over, the one named last changes fastest.
Arguments:
- tokens: bfloat16 [2, 5120, 768], P('wa', 'seq'), may hold values from -6 to 6
- cotangent: bfloat16 [2, 5120, 768], P('wa', 'seq'), may hold values from -6 to 6
- w_qkv: bfloat16 [3, 768, 768], P(None, None, 'wa'), may hold values from -0.21875 to 0.21875
- w_out: bfloat16 [768, 768], P('wa'), may hold values from -0.875 to 0.875
- w_up: bfloat16 [768, 3072], P(None, 'wa'), may hold values from -0.21875 to 0.21875
- w_down: bfloat16 [3072, 768], P('wa'), may hold values from -0.109375 to 0.109375
- gain_attn: bfloat16 [768], P('wa'), may hold values from 0.25 to 1.75
- gain_mlp: bfloat16 [768], P('wa'), may hold values from 0.25 to 1.75
- router: bfloat16 [768], P('wa'), may hold values from -0.21875 to 0.21875
- picked: int32 [2, 1280], replicated, may hold values from 0 to 319, as said below
- counts: int32 [2, 16], replicated, may hold values from 1 to 80, as said below
Outputs:
- mixed: bfloat16 [2, 5120, 768], P('wa', 'seq')
- grad_tokens: bfloat16 [2, 5120, 768], P('wa', 'seq')
- grad_qkv: float32 [3, 768, 768], P(None, None, 'wa')
- grad_out: float32 [768, 768], P('wa')
- grad_up: float32 [768, 3072], P(None, 'wa')
- grad_down: float32 [3072, 768], P('wa')
- grad_gain_attn: float32 [768], P('wa')
- grad_gain_mlp: float32 [768], P('wa')
- grad_router: float32 [768], P('wa')
Inputs may be any that keep to these rules, and one draw needn't show every extreme that they name: For stream s and device d, entries d * 80 to d * 80 + counts[s, d] - 1 of picked[s] are the indices of that device's selected tokens within its block; the 80 entries of one device are distinct. `counts`: selected tokens of stream s on device d; in each stream some device has exactly 80.
All inputs are finite; a program needn't handle non-finite values.
Results may differ from a plain program's by a relative error of at most 0.014.
The roundings to bfloat16 on the way count: a program that leaves them out, or rounds other values in their place, can miss the bound.
Values may be sent and summed in bfloat16 or wider, within the bound.
A program may use at most 320 MiB of HBM per device.

v0:
```python
import jax
import jax.numpy as jnp
from jax import lax
from jax.sharding import PartitionSpec as P

HD = 64
CAP = 80
EPS = 1e-05
NEG = -1e30


def norm_rows(value, gain):
    scale = lax.rsqrt(jnp.mean(value * value, axis=-1, keepdims=True) + EPS)
    return (value * scale * gain, scale)


def norm_back(value, scale, gain, grad_out):
    normed = value * scale
    weighted = grad_out * gain
    grad_value = scale * (weighted - normed * jnp.mean(weighted * normed, axis=-1, keepdims=True))
    return (grad_value, normed)


def gelu_back(pre, grad):
    unused, pull = jax.vjp(lambda value: jax.nn.gelu(value, approximate=True), pre)
    return pull(grad)[0]


def body(
    tokens, cotangent, w_qkv, w_out, w_up, w_down, gain_attn, gain_mlp, router, picked, counts
):
    f32 = jnp.float32
    bf16 = jnp.bfloat16
    nseq = lax.axis_size("seq")
    me = lax.axis_index("seq")
    side = lax.axis_index("wa")
    slots = jnp.arange(CAP, dtype=jnp.int32)
    own_rows = lax.dynamic_slice(picked, (side, me * CAP), (1, CAP))[0]
    x_own = jnp.take(tokens[0], own_rows, axis=0)
    dy_own = jnp.take(cotangent[0], own_rows, axis=0).astype(f32)
    x_rows, g_attn, g_mlp, w_router = (
        lax.all_gather(x_own[None], "wa", axis=0, tiled=True),
        lax.all_gather(gain_attn, "wa", axis=0, tiled=True),
        lax.all_gather(gain_mlp, "wa", axis=0, tiled=True),
        lax.all_gather(router, "wa", axis=0, tiled=True),
    )
    qkv_w, out_w, up_w, down_w = (w_qkv, w_out, w_up, w_down)
    streams = jnp.arange(lax.axis_size("wa"))
    stream_picked = jnp.take(picked, streams, axis=0)
    stream_counts = jnp.take(counts, streams, axis=0)
    key_index = jnp.arange(nseq * CAP, dtype=jnp.int32)
    key_device = key_index // CAP
    key_pos = stream_picked * nseq + key_device[None, :]
    key_live = (key_index % CAP)[None, :] < jnp.take(stream_counts, key_device, axis=1)
    query_index = me * CAP + slots
    query_pos = lax.dynamic_slice_in_dim(key_pos, me * CAP, CAP, 1)
    own_live = (slots < counts[side, me]).astype(f32)
    gains_a = g_attn.astype(f32)
    gains_m = g_mlp.astype(f32)
    x_keep = x_own.astype(f32)
    weight = jax.nn.sigmoid(jnp.dot(x_own, w_router, preferred_element_type=f32))
    x_wide = x_rows.astype(f32)
    normed_a, scale_a = norm_rows(x_wide, gains_a)
    u_rows = normed_a.astype(bf16)
    qkv = jnp.einsum("srd,cde->csre", u_rows, qkv_w, preferred_element_type=f32).astype(bf16)
    query = qkv[0]
    local_kv = qkv[1:]
    batch = query.shape[0]
    heads = query.shape[-1] // HD
    factor = HD ** (-0.5)
    split_q = query.reshape(batch, CAP, heads, HD)
    kv_all = lax.all_gather(local_kv, "seq", axis=2, tiled=True)
    block = 8 * CAP
    nblock = kv_all.shape[2] // block

    def block_of(start):
        keys_b = lax.dynamic_slice_in_dim(kv_all[0], start, block, 1).reshape(
            batch, block, heads, HD
        )
        vals_b = lax.dynamic_slice_in_dim(kv_all[1], start, block, 1).reshape(
            batch, block, heads, HD
        )
        k_pos = lax.dynamic_slice_in_dim(key_pos, start, block, 1)
        k_live = lax.dynamic_slice_in_dim(key_live, start, block, 1)
        k_index = start + jnp.arange(block, dtype=jnp.int32)
        allowed = (k_pos[:, None, :] <= query_pos[:, :, None]) & (
            k_live[:, None, :] | (k_index[None, None, :] == query_index[None, :, None])
        )
        raw = jnp.einsum("sqhd,skhd->shqk", split_q, keys_b, preferred_element_type=f32) * factor
        return (keys_b, vals_b, allowed, jnp.where(allowed[:, None], raw, NEG))

    def max_sum(number, carry):
        top, total = carry
        unused_k, unused_v, allowed, scores = block_of(number * block)
        new_top = jnp.maximum(top, jnp.max(scores, axis=-1, keepdims=True))
        expd = jnp.where(allowed[:, None], jnp.exp(scores - new_top), 0.0)
        return (new_top, total * jnp.exp(top - new_top) + jnp.sum(expd, axis=-1, keepdims=True))

    top_start = jnp.full((batch, heads, CAP, 1), NEG, f32)
    top, total = lax.fori_loop(
        0, nblock, max_sum, (top_start, jnp.zeros((batch, heads, CAP, 1), f32))
    )
    lse = top + jnp.log(total)

    def weigh(number, acc):
        unused_k, vals_b, allowed, scores = block_of(number * block)
        probs_low = jnp.exp(scores - lse).astype(bf16)
        return acc + jnp.einsum("shqk,skhd->sqhd", probs_low, vals_b, preferred_element_type=f32)

    acc = lax.fori_loop(0, nblock, weigh, jnp.zeros((batch, CAP, heads, HD), f32))
    attended = acc.reshape(query.shape).astype(bf16)
    attn_part = jnp.einsum("sqe,ed->sqd", attended, out_w, preferred_element_type=f32)
    attn_own = lax.psum_scatter(attn_part, "wa", scatter_dimension=0, tiled=True)[0]
    resid = x_keep + attn_own
    normed_m, scale_m = norm_rows(resid, gains_m)
    w_own = normed_m.astype(bf16)
    w_rows = lax.all_gather(w_own[None], "wa", axis=0, tiled=True)
    pre = jnp.einsum("srd,df->srf", w_rows, up_w, preferred_element_type=f32)
    act = jax.nn.gelu(pre, approximate=True).astype(bf16)
    mlp_part = jnp.einsum("srf,fd->srd", act, down_w, preferred_element_type=f32)
    mlp_own = lax.psum_scatter(
        mlp_part.astype(jnp.bfloat16), "wa", scatter_dimension=0, tiled=True
    ).astype(jnp.float32)[0]
    branch = attn_own + mlp_own
    lift = (weight * own_live)[:, None]
    out_rows = (x_keep + lift * branch).astype(bf16)
    mixed_out = tokens.at[0, own_rows].set(out_rows)
    grad_branch = dy_own * lift
    grad_logit = jnp.sum(dy_own * branch, axis=-1) * own_live * weight * (1.0 - weight)
    grad_router = jnp.dot(grad_logit, x_keep, precision=lax.Precision.HIGHEST)
    grad_m = grad_branch.astype(bf16)
    grad_m_rows = lax.all_gather(grad_m[None], "wa", axis=0, tiled=True)
    grad_down = jnp.einsum("srf,srd->fd", act, grad_m_rows, preferred_element_type=f32)
    grad_act = jnp.einsum("srd,fd->srf", grad_m_rows, down_w, preferred_element_type=f32)
    grad_pre = gelu_back(pre, grad_act).astype(bf16)
    grad_up = jnp.einsum("srd,srf->df", w_rows, grad_pre, preferred_element_type=f32)
    grad_w_part = jnp.einsum("srf,df->srd", grad_pre, up_w, preferred_element_type=f32)
    grad_w_own = lax.psum_scatter(grad_w_part, "wa", scatter_dimension=0, tiled=True)[0]
    grad_resid, hat_m = norm_back(resid, scale_m, gains_m, grad_w_own)
    grad_gain_m = jnp.sum(grad_w_own * hat_m, axis=0)
    grad_a = (grad_branch + grad_resid).astype(bf16)
    grad_a_rows = lax.all_gather(grad_a[None], "wa", axis=0, tiled=True)
    grad_out = jnp.einsum("sqe,sqd->ed", attended, grad_a_rows, preferred_element_type=f32)
    grad_attended = jnp.einsum(
        "sqd,ed->sqe", grad_a_rows, out_w, preferred_element_type=f32
    ).astype(bf16)
    split_do = grad_attended.reshape(batch, CAP, heads, HD)

    def delta_step(number, delta):
        unused_k, vals_b, allowed, scores = block_of(number * block)
        probs = jnp.exp(scores - lse)
        grad_probs = jnp.einsum("sqhd,skhd->shqk", split_do, vals_b, preferred_element_type=f32)
        return delta + jnp.sum(grad_probs * probs, axis=-1, keepdims=True)

    delta = lax.fori_loop(0, nblock, delta_step, jnp.zeros((batch, heads, CAP, 1), f32))

    def grad_step(number, carry):
        grad_query, holder = carry
        start = number * block
        keys_b, vals_b, allowed, scores = block_of(start)
        probs = jnp.exp(scores - lse)
        grad_probs = jnp.einsum("sqhd,skhd->shqk", split_do, vals_b, preferred_element_type=f32)
        grad_scores = (probs * (grad_probs - delta)).astype(bf16)
        grad_query = (
            grad_query
            + jnp.einsum("shqk,skhd->sqhd", grad_scores, keys_b, preferred_element_type=f32)
            * factor
        )
        grad_keys = (
            jnp.einsum("shqk,sqhd->skhd", grad_scores, split_q, preferred_element_type=f32) * factor
        )
        grad_values = jnp.einsum(
            "shqk,sqhd->skhd", probs.astype(bf16), split_do, preferred_element_type=f32
        )
        paired = jnp.stack([grad_keys, grad_values]).reshape(2, batch, block, heads * HD)
        holder = lax.dynamic_update_slice_in_dim(holder, paired, start, 2)
        return (grad_query, holder)

    grad_query, holder = lax.fori_loop(
        0,
        nblock,
        grad_step,
        (jnp.zeros((batch, CAP, heads, HD), f32), jnp.zeros(kv_all.shape, f32)),
    )
    kv_total = lax.psum_scatter(holder.astype(bf16), "seq", scatter_dimension=2, tiled=True)
    grad_qkv_rows = jnp.concatenate(
        [grad_query.reshape(query.shape)[None].astype(bf16), kv_total.astype(bf16)], axis=0
    )
    grad_qkv = jnp.einsum("srd,csre->cde", u_rows, grad_qkv_rows, preferred_element_type=f32)
    grad_u_part = jnp.einsum("csre,cde->srd", grad_qkv_rows, qkv_w, preferred_element_type=f32)
    part_gain_a = jnp.sum(grad_u_part * (x_wide * scale_a), axis=(0, 1))
    grad_u_all, grad_gain_a, grad_gain_m, grad_router = (
        lax.psum_scatter(
            grad_u_part.astype(jnp.bfloat16), "wa", scatter_dimension=0, tiled=True
        ).astype(jnp.float32),
        lax.psum_scatter(
            part_gain_a.astype(jnp.bfloat16), "wa", scatter_dimension=0, tiled=True
        ).astype(jnp.float32),
        lax.psum_scatter(
            grad_gain_m.astype(jnp.bfloat16), "wa", scatter_dimension=0, tiled=True
        ).astype(jnp.float32),
        lax.psum_scatter(
            grad_router.astype(jnp.bfloat16), "wa", scatter_dimension=0, tiled=True
        ).astype(jnp.float32),
    )
    grad_u_own = grad_u_all[0]
    grad_x_norm, unused = norm_back(x_keep, scale_a[side], gains_a, grad_u_own)
    grad_rows = grad_x_norm + grad_resid + grad_logit[:, None] * w_router.astype(f32)[None, :]
    grad_tokens = cotangent.astype(f32).at[0, own_rows].add(grad_rows).astype(bf16)
    shares = (grad_qkv, grad_out, grad_up, grad_down, grad_gain_a, grad_gain_m, grad_router)
    large = lax.psum(tuple((share.astype(bf16) for share in shares[:4])), "seq")
    small = lax.psum(shares[4:], "seq")
    summed = tuple((part.astype(f32) for part in large)) + small
    return (
        mixed_out,
        grad_tokens,
        summed[0],
        summed[1],
        summed[2],
        summed[3],
        summed[4],
        summed[5],
        summed[6],
    )


def solution(mesh):
    return jax.shard_map(
        body,
        mesh=mesh,
        in_specs=(
            P("wa", "seq", None),
            P("wa", "seq", None),
            P(None, None, "wa"),
            P("wa", None),
            P(None, "wa"),
            P("wa", None),
            P("wa"),
            P("wa"),
            P("wa"),
            P(),
            P(),
        ),
        out_specs=(
            P("wa", "seq", None),
            P("wa", "seq", None),
            P(None, None, "wa"),
            P("wa", None),
            P(None, "wa"),
            P("wa", None),
            P("wa"),
            P("wa"),
            P("wa"),
        ),
        check_vma=False,
    )
```

profile of v0, /device:TPU:0, one launch (start us, length us, event | category | flops | bytes accessed | tf_op | source)
XLA Modules:
  0.0 643.2 jit_solution(9726516830229339342)
XLA Ops:
  10.8 2.1 all-gather
  12.8 1.8 all-gather.5
  15.4 2.0 fusion.59
  21.3 3.2 gather_fusion.2
  24.5 1.9 fusion.78
  27.7 68.0 %all-gather.9.cloned.1.call-done = bf16[2,2,1280,384]{3,2,0,1:T(8,128)(2,1)} async-done(((bf16[2,2,80,384]{3,2,0,1:T(8,128)(2,1)}), bf16[2,2,1280,384]{3,2,0,1:T(8,128)(2,1)}) %all-gather.9.cloned.1.call-update) | async-done | bytes 3932176 | tf_op jit(solution)/shard_map/all_gather | solution.py:72
  95.6 6.3 copy.65
  101.9 14.6 %while.60 = (s32[]{:T(128)}, f32[2,6,80,1]{2,1,0,3:T(8,128)S(1)}, f32[2,6,80,1]{2,1,0,3:T(8,128)S(1)}, s32[2,1280]{1,0:T(2,128)S(1)}, s32[2,80]{1,0:T(2,128)S(1)...) while((s32[]{:T(128)}, f32[2,6,80,1]{2,1,0,3:T(8,128)S(1)}, ...), condition=%wide.region_4.6_spmd.clone, body=%wide.region_1.0_spmd.clone.sunk | while | flops 83922328 | bytes 12404690 | solution.py:100
  104.6 2.0 fusion.198
  106.7 2.5 select_reduce_fusion.2
  111.9 2.0 fusion.198
  114.0 2.5 select_reduce_fusion.2
  117.1 23.4 %while.61 = (s32[]{:T(128)}, f32[2,80,6,64]{1,3,2,0:T(8,128)}, bf16[2,2,1280,384]{2,3,1,0:T(8,128)(2,1)}, s32[2,1280]{1,0:T(2,128)S(1)}, s32[2,80]{1,0:T(2,128)S...) while((s32[]{:T(128)}, f32[2,80,6,64]{1,3,2,0:T(8,128)}, ...), condition=%wide.region_6.8_spmd.clone, body=%wide.region_5.7_spmd.clone.sunk | while | flops 160226000 | bytes 14713809 | solution.py:110
  117.1 4.3 fusion.202
  121.4 2.6 constant_dynamic-slice_fusion.31
  125.6 3.2 fusion.203
  128.8 4.3 fusion.202
  133.1 2.6 constant_dynamic-slice_fusion.31
  137.3 3.3 fusion.203
  142.3 2.2 fusion.80
  153.2 2.1 all-gather.2
  157.5 2.0 all-gather.1
  159.5 2.3 fusion.45
  164.3 2.6 fusion.75
  170.6 11.8 %reduce-scatter.10.cloned.1.call-done = f32[1,80,768]{2,1,0:T(8,128)} async-done(((f32[2,80,768]{2,1,0:T(8,128)}), f32[1,80,768]{2,1,0:T(8,128)}) %reduce-scatter.10.cloned.1.call-update) | async-done | bytes 245776 | tf_op jit(solution)/shard_map/reduce_scatter | solution.py:138
  182.4 1.9 fusion.102
  185.4 2.2 all-gather.3
  188.3 15.5 %while.62 = (s32[]{:T(128)}, f32[2,6,80,1]{2,0,1,3:T(2,128)S(1)}, bf16[2,2,1280,384]{2,3,1,0:T(8,128)(2,1)}, bf16[2,80,6,64]{1,3,2,0:T(8,128)(2,1)S(1)}, s32[2,1...) while((s32[]{:T(128)}, f32[2,6,80,1]{2,0,1,3:T(2,128)S(1)}, ...), condition=%wide.region_15.17_spmd.clone, body=%wide.region_13.16_spmd.clone.sunk | while | flops 160718496 | bytes 19275736 | solution.py:155
  188.3 3.7 fusion.208
  196.0 3.7 fusion.208
  203.7 2.3 broadcast_in_dim.274.clone
  206.0 34.5 %while.63 = (s32[]{:T(128)}, f32[2,80,6,64]{1,3,2,0:T(8,128)S(1)}, bf16[2,2,1280,384]{3,2,0,1:T(8,128)(2,1)}, bf16[2,2,1280,384]{2,3,1,0:T(8,128)(2,1)}, s32[2,1...) while((s32[]{:T(128)}, f32[2,80,6,64]{1,3,2,0:T(8,128)S(1)}, ...), condition=%wide.region_17.19_spmd.clone, body=%wide.region_16.18_spmd.clone.sunk | while | flops 401869536 | bytes 60658212 | solution.py:179
  206.0 4.3 fusion.221
  218.9 2.8 copy.95
  223.3 4.3 fusion.221
  236.2 2.8 copy.95
  241.7 2.2 bitcast_convert_fusion.1
  243.9 2.4 bitcast_convert_fusion
  248.2 128.4 %reduce-scatter.12.cloned.1.call-done = bf16[2,2,80,384]{3,2,0,1:T(8,128)(2,1)} async-done(((bf16[2,2,1280,384]{3,2,0,1:T(8,128)(2,1)}), bf16[2,2,80,384]{3,2,0,1:T(8,128)(2,1)}) %reduce-scatter.12.cloned.1.call-update) | async-done | bytes 245776 | tf_op jit(solution)/shard_map/reduce_scatter | solution.py:185
  376.6 2.4 fusion.85
  380.3 1.9 fusion.51
  387.3 2.5 all-reduce.6
  390.0 43.3 %all-reduce.4 = (f32[384]{0:T(512)}, f32[384]{0:T(512)}, f32[384]{0:T(512)}) all-reduce(f32[384]{0:T(512)S(1)} %dynamic-slice_convert_fusion.2, f32[384]{0:T(512)S(1)} %get-tuple-element.1100, f32[384]{0:T(512)S(1)} %get-tuple-element.1099), channel_id=1, replica_groups=mesh['seq'=16,'wa'=2] {'seq'}, use_global_device_ids=true, to_apply=%region_29.31 | all-reduce | flops 1152 | bytes 9216 | tf_op jit(solution)/shard_map/psum | solution.py:212
  434.4 2.1 scatter_custom_fusion.1
  437.4 186.6 %all-reduce.9.cloned.1.call-done = (bf16[3,768,384]{1,2,0:T(8,128)(2,1)}, bf16[384,768]{1,0:T(8,128)(2,1)}, bf16[768,1536]{1,0:T(8,128)(2,1)}, bf16[1536,768]{1,0:T(8,128)(2,1)}) async-done(((bf16[3,768,384]{1,2,0:T(8,128)(2,1)}, bf16[384,768]{1,0:T(8,128)(2,1)}, bf16[768,1536]{1,0:T(8,128)(2,1)}, bf16[1536,768]{1,0:T(8,128)(2,1)}), (bf16[3,768,384]{1,2,0:T(8,128)(2,1)}, bf16[384,768]{1,0:T(8,128)(2,1)}, ...) | async-done | bytes 7077904 | tf_op jit(solution)/shard_map/psum | solution.py:211
  624.0 4.1 copy.77
  629.2 4.6 convert_element_type.183
  633.8 2.5 convert_element_type.185
  (303 shorter events, 78.5 us)
Async XLA Ops:
  7.2 155.6 %copy-start = (bf16[1536,768]{1,0:T(8,128)(2,1)S(1)}, bf16[1536,768]{1,0:T(8,128)(2,1)}, u32[]{:S(2)}) copy-start(bf16[1536,768]{1,0:T(8,128)(2,1)} %param.26) | copy-start | bytes 7077892
  7.2 5.6 copy-start.59
  7.2 88.4 %all-gather.9.cloned.1.call-start = ((), (), s32[]{:S(2)}) async-start(), calls=%async_computation.5 | async-start | bytes 4177920 | tf_op jit(solution)/shard_map/all_gather | solution.py:72
  8.4 10.5 %copy-start.10 = (bf16[1,320,768]{2,1,0:T(8,128)(2,1)}, bf16[1,320,768]{2,1,0:T(8,128)(2,1)S(1)}, u32[]{:S(2)}) copy-start(bf16[1,320,768]{2,1,0:T(8,128)(2,1)S(1)} %copy.134) | copy-start | bytes 1474564
  9.2 5.5 copy-start.43
  9.2 10.8 %copy-start.35 = (s32[2,1280]{1,0:T(2,128)S(1)}, s32[2,1280]{1,0:T(2,128)}, u32[]{:S(2)}) copy-start(s32[2,1280]{1,0:T(2,128)} %param.30) | copy-start | bytes 30724
  10.0 16.5 %copy-start.4 = (bf16[80,768]{1,0:T(8,128)(2,1)}, bf16[80,768]{1,0:T(8,128)(2,1)S(1)}, u32[]{:S(2)}) copy-start(bf16[80,768]{1,0:T(8,128)(2,1)S(1)} %gather_fusion.3) | copy-start | bytes 368644
  10.0 10.6 %copy-start.42 = (s32[2,16]{1,0:T(2,128)S(1)}, s32[2,16]{1,0:T(2,128)}, u32[]{:S(2)}) copy-start(s32[2,16]{1,0:T(2,128)} %param.31) | copy-start | bytes 388
  12.8 14.5 %copy-start.20 = (bf16[160,768]{1,0:T(8,128)(2,1)}, bf16[160,768]{1,0:T(8,128)(2,1)S(1)}, u32[]{:S(2)}) copy-start(bf16[160,768]{1,0:T(8,128)(2,1)S(1)} %all-gather) | copy-start | bytes 737284
  14.7 12.8 %copy-start.40 = (f32[768]{0:T(1024)}, f32[768]{0:T(1024)S(1)}, u32[]{:S(2)}) copy-start(f32[768]{0:T(1024)S(1)} %reshape.509) | copy-start | bytes 9220
  18.9 136.3 %reduce-scatter.6.cloned.1.call-start = ((), (), s32[]{:S(2)}) async-start(), calls=%async_computation.6 | async-start | bytes 737280 | tf_op jit(solution)/shard_map/reduce_scatter | solution.py:113
  140.6 8.5 %copy-start.8 = (bf16[1,320,768]{2,1,0:T(8,128)(2,1)S(1)}, bf16[1,320,768]{2,1,0:T(8,128)(2,1)}, u32[]{:S(2)}) copy-start(bf16[1,320,768]{2,1,0:T(8,128)(2,1)} %param.22) | copy-start | bytes 1474564
  140.6 11.1 %copy-start.31 = (bf16[80,768]{1,0:T(8,128)(2,1)S(1)}, bf16[80,768]{1,0:T(8,128)(2,1)}, u32[]{:S(2)}) copy-start(bf16[80,768]{1,0:T(8,128)(2,1)} %copy-done.30) | copy-start | bytes 368644
  140.6 12.5 %copy-start.44 = (pred[80]{0:T(512)(128)(4,1)S(1)}, pred[80]{0:T(512)(128)(4,1)}, u32[]{:S(2)}) copy-start(pred[80]{0:T(512)(128)(4,1)} %copy-done.43) | copy-start | bytes 244
  140.6 14.7 %copy-start.5 = (bf16[80,768]{1,0:T(8,128)(2,1)S(1)}, bf16[80,768]{1,0:T(8,128)(2,1)}, u32[]{:S(2)}) copy-start(bf16[80,768]{1,0:T(8,128)(2,1)} %copy-done.4) | copy-start | bytes 368644
  144.5 26.0 %reduce-scatter.8.cloned.1.call-start = ((), (), s32[]{:S(2)}) async-start(), calls=%async_computation.7 | async-start | bytes 368640 | tf_op jit(solution)/shard_map/reduce_scatter | solution.py:121
  149.9 11.9 %copy-start.24 = (bf16[80,768]{1,0:T(8,128)(2,1)}, bf16[80,768]{1,0:T(8,128)(2,1)S(1)}, u32[]{:S(2)}) copy-start(bf16[80,768]{1,0:T(8,128)(2,1)S(1)} %gather_fusion.4) | copy-start | bytes 368644
  151.7 10.1 %copy-start.46 = (bf16[2,1,384]{2,1,0:T(2,128)(2,1)}, bf16[2,1,384]{2,1,0:T(2,128)(2,1)S(1)}, u32[]{:S(2)}) copy-start(bf16[2,1,384]{2,1,0:T(2,128)(2,1)S(1)} %all-gather.4) | copy-start | bytes 4612
  156.5 27.8 %copy-start.50 = (f32[80]{0:T(128)}, f32[80]{0:T(128)S(1)}, u32[]{:S(2)}) copy-start(f32[80]{0:T(128)S(1)} %add_rsqrt_fusion.1) | copy-start | bytes 964
  159.5 4.7 copy-start.15
  164.2 18.1 %reduce-scatter.10.cloned.1.call-start = ((), (), s32[]{:S(2)}) async-start(), calls=%async_computation.8 | async-start | bytes 737280 | tf_op jit(solution)/shard_map/reduce_scatter | solution.py:138
  167.0 15.4 %copy-start.7 = (f32[1,80,768]{2,1,0:T(8,128)S(1)}, f32[1,80,768]{2,1,0:T(8,128)}, u32[]{:S(2)}) copy-start(f32[1,80,768]{2,1,0:T(8,128)} %reduce-scatter.6.cloned.1.call-done) | copy-start | bytes 737284
  167.0 15.4 %copy-start.25 = (bf16[80,768]{1,0:T(8,128)(2,1)S(1)}, bf16[80,768]{1,0:T(8,128)(2,1)}, u32[]{:S(2)}) copy-start(bf16[80,768]{1,0:T(8,128)(2,1)} %copy-done.24) | copy-start | bytes 368644
  167.0 17.3 %copy-start.54 = (f32[80]{0:T(128)S(1)}, f32[80]{0:T(128)}, u32[]{:S(2)}) copy-start(f32[80]{0:T(128)} %copy-done.53) | copy-start | bytes 964
  167.0 20.6 %copy-start.14 = (bf16[384,768]{1,0:T(8,128)(2,1)S(1)}, bf16[384,768]{1,0:T(8,128)(2,1)}, u32[]{:S(2)}) copy-start(bf16[384,768]{1,0:T(8,128)(2,1)} %param.24) | copy-start | bytes 1769476
  168.7 19.4 %copy-start.38 = (f32[2,6,80,1]{2,1,0,3:T(8,128)S(1)}, f32[2,6,80,1]{2,1,0,3:T(8,128)}, u32[]{:S(2)}) copy-start(f32[2,6,80,1]{2,1,0,3:T(8,128)} %get-tuple-element.1591) | copy-start | bytes 11524
  168.7 207.9 %reduce-scatter.12.cloned.1.call-start = ((), (), s32[]{:S(2)}) async-start(), calls=%async_computation.9 | async-start | bytes 4177920 | tf_op jit(solution)/shard_map/reduce_scatter | solution.py:185
  184.3 4.0 copy-start.56
  240.6 3.4 copy-start.39
  240.6 192.7 %reduce-scatter.14.cloned.1.call-start = ((), (), s32[]{:S(2)}) async-start(), calls=%async_computation.10 | async-start | bytes 368640 | tf_op jit(solution)/shard_map/reduce_scatter | solution.py:193
  243.9 132.7 %copy-start.21 = (bf16[160,768]{1,0:T(8,128)(2,1)S(1)}, bf16[160,768]{1,0:T(8,128)(2,1)}, u32[]{:S(2)}) copy-start(bf16[160,768]{1,0:T(8,128)(2,1)} %copy-done.20) | copy-start | bytes 737284
  243.9 132.7 %copy-start.26 = (bf16[3,768,384]{2,1,0:T(8,128)(2,1)S(1)}, bf16[3,768,384]{2,1,0:T(8,128)(2,1)}, u32[]{:S(2)}) copy-start(bf16[3,768,384]{2,1,0:T(8,128)(2,1)} %param.23) | copy-start | bytes 5308420
  243.9 132.7 %copy-start.49 = (f32[2,80]{1,0:T(2,128)S(1)}, f32[2,80]{1,0:T(2,128)}, u32[]{:S(2)}) copy-start(f32[2,80]{1,0:T(2,128)} %copy-done.48) | copy-start | bytes 1924
  246.4 132.7 %copy-start.19 = (bf16[160,768]{1,0:T(8,128)(2,1)S(1)}, bf16[160,768]{1,0:T(8,128)(2,1)}, u32[]{:S(2)}) copy-start(bf16[160,768]{1,0:T(8,128)(2,1)} %copy-done.18) | copy-start | bytes 737284
  246.4 132.7 %copy-start.28 = (bf16[2,80,6,64]{1,3,2,0:T(8,128)(2,1)S(1)}, bf16[2,80,6,64]{1,3,2,0:T(8,128)(2,1)}, u32[]{:S(2)}) copy-start(bf16[2,80,6,64]{1,3,2,0:T(8,128)(2,1)} %copy-done.27) | copy-start | bytes 368644
  246.4 133.9 %copy-start.41 = (f32[768]{0:T(1024)S(1)}, f32[768]{0:T(1024)}, u32[]{:S(2)}) copy-start(f32[768]{0:T(1024)} %copy-done.40) | copy-start | bytes 9220
  376.6 3.7 copy-start.61
  379.0 245.0 %all-reduce.9.cloned.1.call-start = ((), (), s32[]{:S(2)}) async-start(), calls=%async_computation.11 | async-start | bytes 14155776 | tf_op jit(solution)/shard_map/psum | solution.py:211
  382.2 2.8 copy-start.37
  382.3 4.1 copy-start.58
  382.3 4.1 copy-start.60
  382.3 4.8 copy-start.32
  382.3 52.1 %copy-start.17 = (f32[1,80,768]{2,1,0:T(8,128)S(1)}, f32[1,80,768]{2,1,0:T(8,128)}, u32[]{:S(2)}) copy-start(f32[1,80,768]{2,1,0:T(8,128)} %reduce-scatter.10.cloned.1.call-done) | copy-start | bytes 737284
  382.3 52.1 %copy-start.51 = (f32[80]{0:T(128)S(1)}, f32[80]{0:T(128)}, u32[]{:S(2)}) copy-start(f32[80]{0:T(128)} %copy-done.50) | copy-start | bytes 964
  382.3 52.1 %copy-start.57 = (f32[80]{0:T(128)S(1)}, f32[80]{0:T(128)}, u32[]{:S(2)}) copy-start(f32[80]{0:T(128)} %copy-done.56) | copy-start | bytes 964
  386.4 241.7 %copy-start.12 = (bf16[320,768]{1,0:T(8,128)(2,1)}, bf16[320,768]{1,0:T(8,128)(2,1)S(1)}, u32[]{:S(2)}) copy-start(bf16[320,768]{1,0:T(8,128)(2,1)S(1)} %scatter_custom_fusion) | copy-start | bytes 1474564
  624.0 4.1 copy-start.36
  629.2 4.7 copy-start.13
  (24 other events, 38.7 us)
Sparse Core Ops, SparseCore 0:
  19.1 76.5 all-gather.8
  144.7 6.4 reduce-scatter.5
  164.4 6.1 reduce-scatter.7
  173.3 9.0 reduce-scatter.9
  240.7 135.8 reduce-scatter.11
  379.1 6.7 reduce-scatter.13
  393.0 230.9 all-reduce.8
where the time goes:
time: 645 us; the launch traced here: 643 us
  waiting for transfers between devices  397 us (62%)
  local copies, waits for them, and re-layouts  88.5 us (14%)
  blocking collectives  59.5 us (9%)
  matrix products  44.7 us (7%)
  other arithmetic  37.5 us (6%)
  between operations  15.6 us (2%)
    psum x1, waiting for transfers between devices, body(): large = lax.psum(tuple((share.astype(bf16) for share in shares[:4])), 'seq')  187 us
    reduce_scatter x1, waiting for transfers between devices, body(): lax.psum_scatter(holder.astype(bf16), 'seq', scatter_dimension=2, tiled=T...  128 us
    all_gather x1, waiting for transfers between devices, body(): kv_all = lax.all_gather(local_kv, 'seq', axis=2, tiled=True)  68 us
    psum x1, blocking collectives, body(): small = lax.psum(shares[4:], 'seq')  43.3 us
    unnamed x132, local copies, waits for them, and re-layouts  19.9 us
    slice x6, local copies, waits for them, and re-layouts, block_of(): kv_all[0]  19.3 us
  transfers between devices with their start and end apart: 7, of which 5 were waited for; matrix products, arithmetic and copies ran while one was open for 5% of the time, Pallas kernels for 0%

commit v1 on v0

--- a/solution.py
+++ b/solution.py
@@ -69,7 +69,13 @@
     heads = query.shape[-1] // HD
     factor = HD ** (-0.5)
     split_q = query.reshape(batch, CAP, heads, HD)
-    kv_all = lax.all_gather(local_kv, "seq", axis=2, tiled=True)
+    devices = lax.axis_size("seq")
+    block_2, blocks = (local_kv, [local_kv])
+    for _ in range(devices - 1):
+        block_2 = lax.ppermute(block_2, "seq", [(i, (i + 1) % devices) for i in range(devices)])
+        blocks.insert(0, block_2)
+    row_of_blocks = jnp.concatenate(blocks, axis=2)
+    kv_all = jnp.roll(row_of_blocks, (lax.axis_index("seq") + 1) * local_kv.shape[2], axis=2)
     block = 8 * CAP
     nblock = kv_all.shape[2] // block
 

time: 645 us -> 731 us (1.13)
  waiting for transfers between devices: 397 us -> 474 us
    ppermute x0 -> x15, waiting for transfers between devices: none -> 149 us  [body(): lax.ppermute(block_2, 'seq', [(i, (i + 1) % devices) for i in range(devic...]
    all_gather x1 -> x0, waiting for transfers between devices: 68 us -> none  [body(): kv_all = lax.all_gather(local_kv, 'seq', axis=2, tiled=True)]
    unnamed x132 -> x205, local copies, waits for them, and re-layouts: 19.9 us -> 37.9 us
  transfers between devices with their start and end apart: 7 -> 21, of which waited for: 5 -> 18; matrix products, arithmetic and copies ran while one was open for 5% -> 5% of each run, Pallas kernels for 0% -> 0%
where the time goes in v1:
time: 731 us; the launch traced here: 729 us
  waiting for transfers between devices  474 us (65%)
  local copies, waits for them, and re-layouts  92.5 us (13%)
  blocking collectives  59.6 us (8%)
  matrix products  44.9 us (6%)
  other arithmetic  37.6 us (5%)
  between operations  16 us (2%)
    psum x1, waiting for transfers between devices, body(): large = lax.psum(tuple((share.astype(bf16) for share in shares[:4])), 'seq')  186 us
    ppermute x15, waiting for transfers between devices, body(): lax.ppermute(block_2, 'seq', [(i, (i + 1) % devices) for i in range(devic...  149 us
    reduce_scatter x1, waiting for transfers between devices, body(): lax.psum_scatter(holder.astype(bf16), 'seq', scatter_dimension=2, tiled=T...  128 us
    psum x1, blocking collectives, body(): small = lax.psum(shares[4:], 'seq')  43.4 us
    unnamed x205, local copies, waits for them, and re-layouts  37.9 us
  transfers between devices with their start and end apart: 21, of which 18 were waited for; matrix products, arithmetic and copies ran while one was open for 5% of the time, Pallas kernels for 0%

profile of v1, /device:TPU:0, one launch (start us, length us, event | category | flops | bytes accessed | tf_op | source)
XLA Modules:
  0.0 728.7 jit_solution(9952614033133106087)
XLA Ops:
  17.2 2.9 collective-permute-start
  20.1 10.3 %collective-permute-done = bf16[2,2,80,384]{3,2,0,1:T(8,128)(2,1)S(1)} collective-permute-done((bf16[2,2,80,384]{3,2,0,1:T(8,128)(2,1)S(1)}, bf16[2,2,80,384]{3,2,0,1:T(8,128)(2,1)S(1)}, u32[]{:S(2)}, u32[]{:S(2)}) %collective-permute-start) | collective-permute-done | bytes 245792 | tf_op jit(solution)/shard_map/ppermute | solution.py:75
  31.1 11.1 %collective-permute-done.1 = bf16[2,2,80,384]{3,2,0,1:T(8,128)(2,1)S(1)} collective-permute-done((bf16[2,2,80,384]{3,2,0,1:T(8,128)(2,1)S(1)}, bf16[2,2,80,384]{3,2,0,1:T(8,128)(2,1)S(1)}, u32[]{:S(2)}, u32[]{:S(2)}) %collective-permute-start.1) | collective-permute-done | bytes 245792 | tf_op jit(solution)/shard_map/ppermute | solution.py:75
  42.2 10.3 %collective-permute-done.2 = bf16[2,2,80,384]{3,2,0,1:T(8,128)(2,1)S(1)} collective-permute-done((bf16[2,2,80,384]{3,2,0,1:T(8,128)(2,1)S(1)}, bf16[2,2,80,384]{3,2,0,1:T(8,128)(2,1)S(1)}, u32[]{:S(2)}, u32[]{:S(2)}) %collective-permute-start.2) | collective-permute-done | bytes 245792 | tf_op jit(solution)/shard_map/ppermute | solution.py:75
  52.5 9.8 %collective-permute-done.3 = bf16[2,2,80,384]{3,2,0,1:T(8,128)(2,1)S(1)} collective-permute-done((bf16[2,2,80,384]{3,2,0,1:T(8,128)(2,1)S(1)}, bf16[2,2,80,384]{3,2,0,1:T(8,128)(2,1)S(1)}, u32[]{:S(2)}, u32[]{:S(2)}) %collective-permute-start.3) | collective-permute-done | bytes 245792 | tf_op jit(solution)/shard_map/ppermute | solution.py:75
  63.0 9.8 %collective-permute-done.4 = bf16[2,2,80,384]{3,2,0,1:T(8,128)(2,1)S(1)} collective-permute-done((bf16[2,2,80,384]{3,2,0,1:T(8,128)(2,1)S(1)}, bf16[2,2,80,384]{3,2,0,1:T(8,128)(2,1)S(1)}, u32[]{:S(2)}, u32[]{:S(2)}) %collective-permute-start.4) | collective-permute-done | bytes 245792 | tf_op jit(solution)/shard_map/ppermute | solution.py:75
  73.5 9.8 %collective-permute-done.5 = bf16[2,2,80,384]{3,2,0,1:T(8,128)(2,1)S(1)} collective-permute-done((bf16[2,2,80,384]{3,2,0,1:T(8,128)(2,1)S(1)}, bf16[2,2,80,384]{3,2,0,1:T(8,128)(2,1)S(1)}, u32[]{:S(2)}, u32[]{:S(2)}) %collective-permute-start.5) | collective-permute-done | bytes 245792 | tf_op jit(solution)/shard_map/ppermute | solution.py:75
  84.0 9.8 %collective-permute-done.6 = bf16[2,2,80,384]{3,2,0,1:T(8,128)(2,1)S(1)} collective-permute-done((bf16[2,2,80,384]{3,2,0,1:T(8,128)(2,1)S(1)}, bf16[2,2,80,384]{3,2,0,1:T(8,128)(2,1)S(1)}, u32[]{:S(2)}, u32[]{:S(2)}) %collective-permute-start.6) | collective-permute-done | bytes 245792 | tf_op jit(solution)/shard_map/ppermute | solution.py:75
  94.5 10.7 %collective-permute-done.7 = bf16[2,2,80,384]{3,2,0,1:T(8,128)(2,1)S(1)} collective-permute-done((bf16[2,2,80,384]{3,2,0,1:T(8,128)(2,1)S(1)}, bf16[2,2,80,384]{3,2,0,1:T(8,128)(2,1)S(1)}, u32[]{:S(2)}, u32[]{:S(2)}) %collective-permute-start.7) | collective-permute-done | bytes 245792 | tf_op jit(solution)/shard_map/ppermute | solution.py:75
  105.9 11.9 %collective-permute-done.8 = bf16[2,2,80,384]{3,2,0,1:T(8,128)(2,1)S(1)} collective-permute-done((bf16[2,2,80,384]{3,2,0,1:T(8,128)(2,1)S(1)}, bf16[2,2,80,384]{3,2,0,1:T(8,128)(2,1)S(1)}, u32[]{:S(2)}, u32[]{:S(2)}) %collective-permute-start.8) | collective-permute-done | bytes 245792 | tf_op jit(solution)/shard_map/ppermute | solution.py:75
  118.5 11.8 %collective-permute-done.9 = bf16[2,2,80,384]{3,2,0,1:T(8,128)(2,1)S(1)} collective-permute-done((bf16[2,2,80,384]{3,2,0,1:T(8,128)(2,1)S(1)}, bf16[2,2,80,384]{3,2,0,1:T(8,128)(2,1)S(1)}, u32[]{:S(2)}, u32[]{:S(2)}) %collective-permute-start.9) | collective-permute-done | bytes 245792 | tf_op jit(solution)/shard_map/ppermute | solution.py:75
  131.0 10.6 %collective-permute-done.10 = bf16[2,2,80,384]{3,2,0,1:T(8,128)(2,1)} collective-permute-done((bf16[2,2,80,384]{3,2,0,1:T(8,128)(2,1)S(1)}, bf16[2,2,80,384]{3,2,0,1:T(8,128)(2,1)}, u32[]{:S(2)}, u32[]{:S(2)}) %collective-permute-start.10) | collective-permute-done | bytes 245792 | tf_op jit(solution)/shard_map/ppermute | solution.py:75
  142.3 9.4 %collective-permute-done.11 = bf16[2,2,80,384]{3,2,0,1:T(8,128)(2,1)} collective-permute-done((bf16[2,2,80,384]{3,2,0,1:T(8,128)(2,1)}, bf16[2,2,80,384]{3,2,0,1:T(8,128)(2,1)}, u32[]{:S(2)}, u32[]{:S(2)}) %collective-permute-start.11) | collective-permute-done | bytes 245792 | tf_op jit(solution)/shard_map/ppermute | solution.py:75
  151.8 3.1 gather_fusion.2
  155.0 6.8 collective-permute-done.12
  164.3 7.6 %collective-permute-done.13 = bf16[2,2,80,384]{3,2,0,1:T(8,128)(2,1)} collective-permute-done((bf16[2,2,80,384]{3,2,0,1:T(8,128)(2,1)}, bf16[2,2,80,384]{3,2,0,1:T(8,128)(2,1)}, u32[]{:S(2)}, u32[]{:S(2)}) %collective-permute-start.13) | collective-permute-done | bytes 245792 | tf_op jit(solution)/shard_map/ppermute | solution.py:75
  173.1 8.9 %collective-permute-done.14 = bf16[2,2,80,384]{3,2,0,1:T(8,128)(2,1)} collective-permute-done((bf16[2,2,80,384]{3,2,0,1:T(8,128)(2,1)}, bf16[2,2,80,384]{3,2,0,1:T(8,128)(2,1)}, u32[]{:S(2)}, u32[]{:S(2)}) %collective-permute-start.14) | collective-permute-done | bytes 245792 | tf_op jit(solution)/shard_map/ppermute | solution.py:75
  196.3 3.0 constant_dynamic-slice_fusion.17
  199.2 6.3 copy.65
  205.5 14.6 %while.60 = (s32[]{:T(128)}, f32[2,6,80,1]{2,1,0,3:T(8,128)S(1)}, f32[2,6,80,1]{2,1,0,3:T(8,128)S(1)}, s32[2,1280]{1,0:T(2,128)S(1)}, s32[2,80]{1,0:T(2,128)S(1)...) while((s32[]{:T(128)}, f32[2,6,80,1]{2,1,0,3:T(8,128)S(1)}, ...), condition=%wide.region_4.6_spmd.clone, body=%wide.region_1.0_spmd.clone.sunk | while | flops 83922328 | bytes 12404682 | solution.py:106
  210.2 2.5 select_reduce_fusion.2
  217.5 2.5 select_reduce_fusion.2
  220.7 16.6 %while.61 = (s32[]{:T(128)}, f32[2,80,6,64]{1,3,2,0:T(8,128)}, bf16[2,2,1280,384]{2,3,1,0:T(8,128)(2,1)}, s32[2,1280]{1,0:T(2,128)S(1)}, s32[2,80]{1,0:T(2,128)S...) while((s32[]{:T(128)}, f32[2,80,6,64]{1,3,2,0:T(8,128)}, ...), condition=%wide.region_6.8_spmd.clone, body=%wide.region_5.7_spmd.clone.sunk | while | flops 160226000 | bytes 14713801 | solution.py:116
  222.2 2.4 fusion.203
  225.8 3.2 fusion.204
  230.5 2.4 fusion.203
  234.0 3.3 fusion.204
  261.3 2.6 fusion.75
  265.8 11.1 %reduce-scatter.10.cloned.1.call-done = f32[1,80,768]{2,1,0:T(8,128)} async-done(((f32[2,80,768]{2,1,0:T(8,128)}), f32[1,80,768]{2,1,0:T(8,128)}) %reduce-scatter.10.cloned.1.call-update) | async-done | bytes 245776 | tf_op jit(solution)/shard_map/reduce_scatter | solution.py:144
  282.6 10.5 %while.62 = (s32[]{:T(128)}, f32[2,6,80,1]{2,0,1,3:T(2,128)S(1)}, bf16[2,2,1280,384]{2,3,1,0:T(8,128)(2,1)}, bf16[2,80,6,64]{1,3,2,0:T(8,128)(2,1)S(1)}, s32[2,1...) while((s32[]{:T(128)}, f32[2,6,80,1]{2,0,1,3:T(2,128)S(1)}, ...), condition=%wide.region_15.17_spmd.clone, body=%wide.region_13.16_spmd.clone.sunk | while | flops 160718496 | bytes 19275728 | solution.py:161
  283.6 2.4 fusion.209
  288.8 2.4 fusion.209
  295.4 30.9 %while.63 = (s32[]{:T(128)}, f32[2,80,6,64]{1,3,2,0:T(8,128)S(1)}, bf16[2,2,1280,384]{3,2,0,1:T(8,128)(2,1)}, bf16[2,2,1280,384]{2,3,1,0:T(8,128)(2,1)}, s32[2,1...) while((s32[]{:T(128)}, f32[2,80,6,64]{1,3,2,0:T(8,128)S(1)}, ...), condition=%wide.region_17.19_spmd.clone, body=%wide.region_16.18_spmd.clone.sunk | while | flops 401869536 | bytes 40997348 | solution.py:185
  296.3 2.4 fusion.222
  303.2 4.1 copy.95
  307.2 3.0 constant_dynamic-update-slice_fusion.34
  311.8 2.4 fusion.222
  318.6 4.1 copy.95
  322.7 3.0 constant_dynamic-update-slice_fusion.34
  329.7 2.4 bitcast_convert_fusion
  333.9 128.3 %reduce-scatter.12.cloned.1.call-done = bf16[2,2,80,384]{3,2,0,1:T(8,128)(2,1)} async-done(((bf16[2,2,1280,384]{3,2,0,1:T(8,128)(2,1)}), bf16[2,2,80,384]{3,2,0,1:T(8,128)(2,1)}) %reduce-scatter.12.cloned.1.call-update) | async-done | bytes 245776 | tf_op jit(solution)/shard_map/reduce_scatter | solution.py:191
  462.2 2.4 fusion.85
  472.9 2.5 all-reduce.6
  475.6 43.4 %all-reduce.4 = (f32[384]{0:T(512)}, f32[384]{0:T(512)}, f32[384]{0:T(512)}) all-reduce(f32[384]{0:T(512)S(1)} %dynamic-slice_convert_fusion.2, f32[384]{0:T(512)S(1)} %get-tuple-element.1100, f32[384]{0:T(512)S(1)} %get-tuple-element.1099), channel_id=1, replica_groups=mesh['seq'=16,'wa'=2] {'seq'}, use_global_device_ids=true, to_apply=%region_29.31 | all-reduce | flops 1152 | bytes 9216 | tf_op jit(solution)/shard_map/psum | solution.py:218
  523.1 186.3 %all-reduce.9.cloned.1.call-done = (bf16[3,768,384]{1,2,0:T(8,128)(2,1)}, bf16[384,768]{1,0:T(8,128)(2,1)}, bf16[768,1536]{1,0:T(8,128)(2,1)}, bf16[1536,768]{1,0:T(8,128)(2,1)}) async-done(((bf16[3,768,384]{1,2,0:T(8,128)(2,1)}, bf16[384,768]{1,0:T(8,128)(2,1)}, bf16[768,1536]{1,0:T(8,128)(2,1)}, bf16[1536,768]{1,0:T(8,128)(2,1)}), (bf16[3,768,384]{1,2,0:T(8,128)(2,1)}, bf16[384,768]{1,0:T(8,128)(2,1)}, ...) | async-done | bytes 7077904 | tf_op jit(solution)/shard_map/psum | solution.py:217
  709.4 4.6 convert_element_type.183
  714.1 2.5 convert_element_type.185
  716.6 4.2 copy.77
  (397 shorter events, 118.2 us)
Async XLA Ops:
  7.2 252.6 %copy-start = (bf16[1536,768]{1,0:T(8,128)(2,1)S(1)}, bf16[1536,768]{1,0:T(8,128)(2,1)}, u32[]{:S(2)}) copy-start(bf16[1536,768]{1,0:T(8,128)(2,1)} %param.26) | copy-start | bytes 7077892
  7.2 245.0 %reduce-scatter.6.cloned.1.call-start = ((), (), s32[]{:S(2)}) async-start(), calls=%async_computation.5 | async-start | bytes 737280 | tf_op jit(solution)/shard_map/reduce_scatter | solution.py:119
  8.4 133.2 %copy-start.61 = (s32[2,16]{1,0:T(2,128)S(1)}, s32[2,16]{1,0:T(2,128)}, u32[]{:S(2)}) copy-start(s32[2,16]{1,0:T(2,128)} %param.31) | copy-start | bytes 388
  10.0 162.0 %copy-start.2 = (bf16[80,768]{1,0:T(8,128)(2,1)}, bf16[80,768]{1,0:T(8,128)(2,1)S(1)}, u32[]{:S(2)}) copy-start(bf16[80,768]{1,0:T(8,128)(2,1)S(1)} %gather_fusion.3) | copy-start | bytes 368644
  10.0 153.7 %copy-start.52 = (s32[2,1280]{1,0:T(2,128)S(1)}, s32[2,1280]{1,0:T(2,128)}, u32[]{:S(2)}) copy-start(s32[2,1280]{1,0:T(2,128)} %param.30) | copy-start | bytes 30724
  13.1 138.6 %copy-start.67 = (f32[2,80]{1,0:T(2,128)}, f32[2,80]{1,0:T(2,128)S(1)}, u32[]{:S(2)}) copy-start(f32[2,80]{1,0:T(2,128)S(1)} %add_rsqrt_fusion) | copy-start | bytes 1924
  15.0 157.0 %copy-start.57 = (f32[768]{0:T(1024)}, f32[768]{0:T(1024)S(1)}, u32[]{:S(2)}) copy-start(f32[768]{0:T(1024)S(1)} %reshape.509) | copy-start | bytes 9220
  17.2 13.2 %collective-permute-start = (bf16[2,2,80,384]{3,2,0,1:T(8,128)(2,1)S(1)}, bf16[2,2,80,384]{3,2,0,1:T(8,128)(2,1)S(1)}, u32[]{:S(2)}, u32[]{:S(2)}) collective-permute-start(bf16[2,2,80,384]{3,2,0,1:T(8,128)(2,1)S(1)} %slice.78), channel_id=1, source_target_pairs={{0,2},{2,4},{4,6},{6,8},{8,10},{10,12},{12,14},{14,16},{16,18},{18... | collective-permute-start | bytes 737288 | tf_op jit(solution)/shard_map/ppermute | solution.py:75
  31.1 11.1 %collective-permute-start.1 = (bf16[2,2,80,384]{3,2,0,1:T(8,128)(2,1)S(1)}, bf16[2,2,80,384]{3,2,0,1:T(8,128)(2,1)S(1)}, u32[]{:S(2)}, u32[]{:S(2)}) collective-permute-start(bf16[2,2,80,384]{3,2,0,1:T(8,128)(2,1)S(1)} %collective-permute-done), channel_id=1, source_target_pairs={{0,2},{2,4},{4,6},{6,8},{8,10},{10,12},{12,14},{14,16},{16,18},{18... | collective-permute-start | bytes 737288 | tf_op jit(solution)/shard_map/ppermute | solution.py:75
  42.2 109.5 %copy-start.34 = (bf16[2,2,80,384]{3,2,0,1:T(8,128)(2,1)}, bf16[2,2,80,384]{3,2,0,1:T(8,128)(2,1)S(1)}, u32[]{:S(2)}) copy-start(bf16[2,2,80,384]{3,2,0,1:T(8,128)(2,1)S(1)} %collective-permute-done.1) | copy-start | bytes 737284
  42.2 10.3 %collective-permute-start.2 = (bf16[2,2,80,384]{3,2,0,1:T(8,128)(2,1)S(1)}, bf16[2,2,80,384]{3,2,0,1:T(8,128)(2,1)S(1)}, u32[]{:S(2)}, u32[]{:S(2)}) collective-permute-start(bf16[2,2,80,384]{3,2,0,1:T(8,128)(2,1)S(1)} %collective-permute-done.1), channel_id=1, source_target_pairs={{0,2},{2,4},{4,6},{6,8},{8,10},{10,12},{12,14},{14,16},{16,18},{18... | collective-permute-start | bytes 737288 | tf_op jit(solution)/shard_map/ppermute | solution.py:75
  52.5 132.5 %copy-start.36 = (bf16[2,2,80,384]{3,2,0,1:T(8,128)(2,1)}, bf16[2,2,80,384]{3,2,0,1:T(8,128)(2,1)S(1)}, u32[]{:S(2)}) copy-start(bf16[2,2,80,384]{3,2,0,1:T(8,128)(2,1)S(1)} %collective-permute-done.2) | copy-start | bytes 737284
  52.5 9.8 %collective-permute-start.3 = (bf16[2,2,80,384]{3,2,0,1:T(8,128)(2,1)S(1)}, bf16[2,2,80,384]{3,2,0,1:T(8,128)(2,1)S(1)}, u32[]{:S(2)}, u32[]{:S(2)}) collective-permute-start(bf16[2,2,80,384]{3,2,0,1:T(8,128)(2,1)S(1)} %collective-permute-done.2), channel_id=1, source_target_pairs={{0,2},{2,4},{4,6},{6,8},{8,10},{10,12},{12,14},{14,16},{16,18},{18... | collective-permute-start | bytes 737288 | tf_op jit(solution)/shard_map/ppermute | solution.py:75
  63.0 9.8 %collective-permute-start.4 = (bf16[2,2,80,384]{3,2,0,1:T(8,128)(2,1)S(1)}, bf16[2,2,80,384]{3,2,0,1:T(8,128)(2,1)S(1)}, u32[]{:S(2)}, u32[]{:S(2)}) collective-permute-start(bf16[2,2,80,384]{3,2,0,1:T(8,128)(2,1)S(1)} %collective-permute-done.3), channel_id=1, source_target_pairs={{0,2},{2,4},{4,6},{6,8},{8,10},{10,12},{12,14},{14,16},{16,18},{18... | collective-permute-start | bytes 737288 | tf_op jit(solution)/shard_map/ppermute | solution.py:75
  73.5 9.8 %collective-permute-start.5 = (bf16[2,2,80,384]{3,2,0,1:T(8,128)(2,1)S(1)}, bf16[2,2,80,384]{3,2,0,1:T(8,128)(2,1)S(1)}, u32[]{:S(2)}, u32[]{:S(2)}) collective-permute-start(bf16[2,2,80,384]{3,2,0,1:T(8,128)(2,1)S(1)} %collective-permute-done.4), channel_id=1, source_target_pairs={{0,2},{2,4},{4,6},{6,8},{8,10},{10,12},{12,14},{14,16},{16,18},{18... | collective-permute-start | bytes 737288 | tf_op jit(solution)/shard_map/ppermute | solution.py:75
  84.0 9.8 %collective-permute-start.6 = (bf16[2,2,80,384]{3,2,0,1:T(8,128)(2,1)S(1)}, bf16[2,2,80,384]{3,2,0,1:T(8,128)(2,1)S(1)}, u32[]{:S(2)}, u32[]{:S(2)}) collective-permute-start(bf16[2,2,80,384]{3,2,0,1:T(8,128)(2,1)S(1)} %collective-permute-done.5), channel_id=1, source_target_pairs={{0,2},{2,4},{4,6},{6,8},{8,10},{10,12},{12,14},{14,16},{16,18},{18... | collective-permute-start | bytes 737288 | tf_op jit(solution)/shard_map/ppermute | solution.py:75
  94.5 10.7 %collective-permute-start.7 = (bf16[2,2,80,384]{3,2,0,1:T(8,128)(2,1)S(1)}, bf16[2,2,80,384]{3,2,0,1:T(8,128)(2,1)S(1)}, u32[]{:S(2)}, u32[]{:S(2)}) collective-permute-start(bf16[2,2,80,384]{3,2,0,1:T(8,128)(2,1)S(1)} %collective-permute-done.6), channel_id=1, source_target_pairs={{0,2},{2,4},{4,6},{6,8},{8,10},{10,12},{12,14},{14,16},{16,18},{18... | collective-permute-start | bytes 737288 | tf_op jit(solution)/shard_map/ppermute | solution.py:75
  105.9 11.9 %collective-permute-start.8 = (bf16[2,2,80,384]{3,2,0,1:T(8,128)(2,1)S(1)}, bf16[2,2,80,384]{3,2,0,1:T(8,128)(2,1)S(1)}, u32[]{:S(2)}, u32[]{:S(2)}) collective-permute-start(bf16[2,2,80,384]{3,2,0,1:T(8,128)(2,1)S(1)} %collective-permute-done.7), channel_id=1, source_target_pairs={{0,2},{2,4},{4,6},{6,8},{8,10},{10,12},{12,14},{14,16},{16,18},{18... | collective-permute-start | bytes 737288 | tf_op jit(solution)/shard_map/ppermute | solution.py:75
  118.5 11.8 %collective-permute-start.9 = (bf16[2,2,80,384]{3,2,0,1:T(8,128)(2,1)S(1)}, bf16[2,2,80,384]{3,2,0,1:T(8,128)(2,1)S(1)}, u32[]{:S(2)}, u32[]{:S(2)}) collective-permute-start(bf16[2,2,80,384]{3,2,0,1:T(8,128)(2,1)S(1)} %collective-permute-done.8), channel_id=1, source_target_pairs={{0,2},{2,4},{4,6},{6,8},{8,10},{10,12},{12,14},{14,16},{16,18},{18... | collective-permute-start | bytes 737288 | tf_op jit(solution)/shard_map/ppermute | solution.py:75
  131.0 10.6 %collective-permute-start.10 = (bf16[2,2,80,384]{3,2,0,1:T(8,128)(2,1)S(1)}, bf16[2,2,80,384]{3,2,0,1:T(8,128)(2,1)}, u32[]{:S(2)}, u32[]{:S(2)}) collective-permute-start(bf16[2,2,80,384]{3,2,0,1:T(8,128)(2,1)S(1)} %collective-permute-done.9), channel_id=1, source_target_pairs={{0,2},{2,4},{4,6},{6,8},{8,10},{10,12},{12,14},{14,16},{16,18},{18... | collective-permute-start | bytes 737288 | tf_op jit(solution)/shard_map/ppermute | solution.py:75
  141.6 10.1 %collective-permute-start.11 = (bf16[2,2,80,384]{3,2,0,1:T(8,128)(2,1)}, bf16[2,2,80,384]{3,2,0,1:T(8,128)(2,1)}, u32[]{:S(2)}, u32[]{:S(2)}) collective-permute-start(bf16[2,2,80,384]{3,2,0,1:T(8,128)(2,1)} %collective-permute-done.10), channel_id=1, source_target_pairs={{0,2},{2,4},{4,6},{6,8},{8,10},{10,12},{12,14},{14,16},{16,18},{18... | collective-permute-start | bytes 737288 | tf_op jit(solution)/shard_map/ppermute | solution.py:75
  151.7 10.1 %collective-permute-start.12 = (bf16[2,2,80,384]{3,2,0,1:T(8,128)(2,1)}, bf16[2,2,80,384]{3,2,0,1:T(8,128)(2,1)}, u32[]{:S(2)}, u32[]{:S(2)}) collective-permute-start(bf16[2,2,80,384]{3,2,0,1:T(8,128)(2,1)} %collective-permute-done.11), channel_id=1, source_target_pairs={{0,2},{2,4},{4,6},{6,8},{8,10},{10,12},{12,14},{14,16},{16,18},{18... | collective-permute-start | bytes 737288 | tf_op jit(solution)/shard_map/ppermute | solution.py:75
  161.8 10.1 %collective-permute-start.13 = (bf16[2,2,80,384]{3,2,0,1:T(8,128)(2,1)}, bf16[2,2,80,384]{3,2,0,1:T(8,128)(2,1)}, u32[]{:S(2)}, u32[]{:S(2)}) collective-permute-start(bf16[2,2,80,384]{3,2,0,1:T(8,128)(2,1)} %collective-permute-done.12), channel_id=1, source_target_pairs={{0,2},{2,4},{4,6},{6,8},{8,10},{10,12},{12,14},{14,16},{16,18},{18... | collective-permute-start | bytes 737288 | tf_op jit(solution)/shard_map/ppermute | solution.py:75
  171.9 10.1 %collective-permute-start.14 = (bf16[2,2,80,384]{3,2,0,1:T(8,128)(2,1)}, bf16[2,2,80,384]{3,2,0,1:T(8,128)(2,1)}, u32[]{:S(2)}, u32[]{:S(2)}) collective-permute-start(bf16[2,2,80,384]{3,2,0,1:T(8,128)(2,1)} %collective-permute-done.13), channel_id=1, source_target_pairs={{0,2},{2,4},{4,6},{6,8},{8,10},{10,12},{12,14},{14,16},{16,18},{18... | collective-permute-start | bytes 737288 | tf_op jit(solution)/shard_map/ppermute | solution.py:75
  173.1 14.1 %copy-start.49 = (bf16[2,2,80,384]{3,2,0,1:T(8,128)(2,1)S(1)}, bf16[2,2,80,384]{3,2,0,1:T(8,128)(2,1)}, u32[]{:S(2)}) copy-start(bf16[2,2,80,384]{3,2,0,1:T(8,128)(2,1)} %copy-done.48) | copy-start | bytes 737284
  173.1 17.1 %copy-start.41 = (bf16[2,2,80,384]{3,2,0,1:T(8,128)(2,1)S(1)}, bf16[2,2,80,384]{3,2,0,1:T(8,128)(2,1)}, u32[]{:S(2)}) copy-start(bf16[2,2,80,384]{3,2,0,1:T(8,128)(2,1)} %copy-done.40) | copy-start | bytes 737284
  237.3 15.0 %copy-start.3 = (bf16[80,768]{1,0:T(8,128)(2,1)S(1)}, bf16[80,768]{1,0:T(8,128)(2,1)}, u32[]{:S(2)}) copy-start(bf16[80,768]{1,0:T(8,128)(2,1)} %copy-done.2) | copy-start | bytes 368644
  241.3 24.5 %reduce-scatter.8.cloned.1.call-start = ((), (), s32[]{:S(2)}) async-start(), calls=%async_computation.6 | async-start | bytes 368640 | tf_op jit(solution)/shard_map/reduce_scatter | solution.py:127
  243.8 35.0 %copy-start.59 = (f32[768]{0:T(1024)}, f32[768]{0:T(1024)S(1)}, u32[]{:S(2)}) copy-start(f32[768]{0:T(1024)S(1)} %reshape.510) | copy-start | bytes 9220
  253.4 25.4 %copy-start.69 = (f32[80]{0:T(128)}, f32[80]{0:T(128)S(1)}, u32[]{:S(2)}) copy-start(f32[80]{0:T(128)S(1)} %add_rsqrt_fusion.1) | copy-start | bytes 964
  261.2 15.7 %reduce-scatter.10.cloned.1.call-start = ((), (), s32[]{:S(2)}) async-start(), calls=%async_computation.7 | async-start | bytes 737280 | tf_op jit(solution)/shard_map/reduce_scatter | solution.py:144
  263.9 14.9 %copy-start.73 = (f32[80]{0:T(128)S(1)}, f32[80]{0:T(128)}, u32[]{:S(2)}) copy-start(f32[80]{0:T(128)} %copy-done.72) | copy-start | bytes 964
  264.0 18.0 %copy-start.12 = (bf16[384,768]{1,0:T(8,128)(2,1)S(1)}, bf16[384,768]{1,0:T(8,128)(2,1)}, u32[]{:S(2)}) copy-start(bf16[384,768]{1,0:T(8,128)(2,1)} %param.24) | copy-start | bytes 1769476
  265.7 16.8 %copy-start.55 = (f32[2,6,80,1]{2,1,0,3:T(8,128)S(1)}, f32[2,6,80,1]{2,1,0,3:T(8,128)}, u32[]{:S(2)}) copy-start(f32[2,6,80,1]{2,1,0,3:T(8,128)} %get-tuple-element.1607) | copy-start | bytes 11524
  265.7 196.5 %reduce-scatter.12.cloned.1.call-start = ((), (), s32[]{:S(2)}) async-start(), calls=%async_computation.8 | async-start | bytes 4177920 | tf_op jit(solution)/shard_map/reduce_scatter | solution.py:191
  326.3 192.6 %reduce-scatter.14.cloned.1.call-start = ((), (), s32[]{:S(2)}) async-start(), calls=%async_computation.9 | async-start | bytes 368640 | tf_op jit(solution)/shard_map/reduce_scatter | solution.py:199
  329.7 132.5 %copy-start.19 = (bf16[160,768]{1,0:T(8,128)(2,1)S(1)}, bf16[160,768]{1,0:T(8,128)(2,1)}, u32[]{:S(2)}) copy-start(bf16[160,768]{1,0:T(8,128)(2,1)} %copy-done.18) | copy-start | bytes 737284
  329.7 132.5 %copy-start.24 = (bf16[3,768,384]{2,1,0:T(8,128)(2,1)S(1)}, bf16[3,768,384]{2,1,0:T(8,128)(2,1)}, u32[]{:S(2)}) copy-start(bf16[3,768,384]{2,1,0:T(8,128)(2,1)} %param.23) | copy-start | bytes 5308420
  329.7 132.5 %copy-start.68 = (f32[2,80]{1,0:T(2,128)S(1)}, f32[2,80]{1,0:T(2,128)}, u32[]{:S(2)}) copy-start(f32[2,80]{1,0:T(2,128)} %copy-done.67) | copy-start | bytes 1924
  332.1 132.6 %copy-start.17 = (bf16[160,768]{1,0:T(8,128)(2,1)S(1)}, bf16[160,768]{1,0:T(8,128)(2,1)}, u32[]{:S(2)}) copy-start(bf16[160,768]{1,0:T(8,128)(2,1)} %copy-done.16) | copy-start | bytes 737284
  332.1 132.6 %copy-start.26 = (bf16[2,80,6,64]{1,3,2,0:T(8,128)(2,1)S(1)}, bf16[2,80,6,64]{1,3,2,0:T(8,128)(2,1)}, u32[]{:S(2)}) copy-start(bf16[2,80,6,64]{1,3,2,0:T(8,128)(2,1)} %copy-done.25) | copy-start | bytes 368644
  332.1 133.7 %copy-start.58 = (f32[768]{0:T(1024)S(1)}, f32[768]{0:T(1024)}, u32[]{:S(2)}) copy-start(f32[768]{0:T(1024)} %copy-done.57) | copy-start | bytes 9220
  464.6 244.8 %all-reduce.9.cloned.1.call-start = ((), (), s32[]{:S(2)}) async-start(), calls=%async_computation.10 | async-start | bytes 14155776 | tf_op jit(solution)/shard_map/psum | solution.py:217
  467.9 52.2 %copy-start.15 = (f32[1,80,768]{2,1,0:T(8,128)S(1)}, f32[1,80,768]{2,1,0:T(8,128)}, u32[]{:S(2)}) copy-start(f32[1,80,768]{2,1,0:T(8,128)} %reduce-scatter.10.cloned.1.call-done) | copy-start | bytes 737284
  467.9 52.2 %copy-start.60 = (f32[768]{0:T(1024)S(1)}, f32[768]{0:T(1024)}, u32[]{:S(2)}) copy-start(f32[768]{0:T(1024)} %copy-done.59) | copy-start | bytes 9220
  467.9 52.2 %copy-start.70 = (f32[80]{0:T(128)S(1)}, f32[80]{0:T(128)}, u32[]{:S(2)}) copy-start(f32[80]{0:T(128)} %copy-done.69) | copy-start | bytes 964
  467.9 52.2 %copy-start.76 = (f32[80]{0:T(128)S(1)}, f32[80]{0:T(128)}, u32[]{:S(2)}) copy-start(f32[80]{0:T(128)} %copy-done.75) | copy-start | bytes 964
  472.0 242.1 %copy-start.10 = (bf16[320,768]{1,0:T(8,128)(2,1)}, bf16[320,768]{1,0:T(8,128)(2,1)S(1)}, u32[]{:S(2)}) copy-start(bf16[320,768]{1,0:T(8,128)(2,1)S(1)} %scatter_custom_fusion) | copy-start | bytes 1474564
  (55 other events, 236.4 us)
Sparse Core Ops, SparseCore 0:
  241.4 3.7 reduce-scatter.5
  261.3 3.5 reduce-scatter.7
  267.8 9.0 reduce-scatter.9
  326.4 135.6 reduce-scatter.11
  464.8 6.7 reduce-scatter.13
  478.4 230.9 all-reduce.8
